TPU v7x, 32 devices: a whole 2x2x4 slice. The times are simulated.
32 devices in a mesh: batch: 8 (over y, x, core), head: 4 (over z).
Axes of the slice: x: 2, y: 2, z: 4, core: 2. Of those that a mesh axis runs over, the one named last changes fastest.
Arguments:
- layer_input: bfloat16 [16384, 768], P(('batch', 'head')), may hold values from -6 to 6
- memory_flags: int32 [32], P('batch'), may hold values 0 or 1
- document_start: int32 [32], P('batch'), may hold values from 1 to 511
- memory_coefficients: bfloat16 [32, 256, 768], P('batch'), may hold values from -6 to 6
- first_gain: bfloat16 [768], replicated, may hold values from 0.5 to 1.5
- first_shift: bfloat16 [768], replicated, may hold values from -1 to 1
- query_weight: bfloat16 [768, 768], P(None, 'head'), may hold values from -0.3125 to 0.3125
- query_bias: bfloat16 [768], P('head'), may hold values from -1 to 1
- key_matrix: bfloat16 [768, 768], P(None, 'head'), may hold values from -0.21875 to 0.21875
- value_matrix: bfloat16 [768, 768], P(None, 'head'), may hold values from -0.21875 to 0.21875
- value_offset_bias: bfloat16 [768], P('head'), may hold values from -1 to 1
- out_weight: bfloat16 [768, 768], P('head'), may hold values from -0.875 to 0.875
- out_bias: bfloat16 [768], replicated, may hold values from -1 to 1
- second_gain: bfloat16 [768], replicated, may hold values from 0.5 to 1.5
- second_shift: bfloat16 [768], replicated, may hold values from -1 to 1
- up_weight: bfloat16 [768, 3072], P(None, 'head'), may hold values from -0.21875 to 0.21875
- up_bias: bfloat16 [3072], P('head'), may hold values from -1 to 1
- down_weight: bfloat16 [3072, 768], P('head'), may hold values from -0.109375 to 0.109375
- down_bias: bfloat16 [768], replicated, may hold values from -1 to 1
- centre_weight: float32 [12, 256], P('head'), may hold values from -0.375 to 0.375
- width_weight: float32 [12, 256], P('head'), may hold values from -0.375 to 0.375
- grad_output: bfloat16 [16384, 768], P(('batch', 'head')), may hold values from -6 to 6
Outputs:
- layer_output: bfloat16 [16384, 768], P(('batch', 'head'))
- input_grad: bfloat16 [16384, 768], P(('batch', 'head'))
- first_gain_grad: float32 [768], replicated
- first_shift_grad: float32 [768], replicated
- query_weight_grad: float32 [768, 768], P(None, 'head')
- query_bias_grad: float32 [768], P('head')
- key_weight_grad: float32 [768, 768], P(None, 'head')
- value_weight_grad: float32 [768, 768], P(None, 'head')
- value_bias_grad: float32 [768], P('head')
- out_weight_grad: float32 [768, 768], P('head')
- out_bias_grad: float32 [768], replicated
- second_gain_grad: float32 [768], replicated
- second_shift_grad: float32 [768], replicated
- up_weight_grad: float32 [768, 3072], P(None, 'head')
- up_bias_grad: float32 [3072], P('head')
- down_weight_grad: float32 [3072, 768], P('head')
- down_bias_grad: float32 [768], replicated
- centre_weight_grad: float32 [12, 256], P('head')
- width_weight_grad: float32 [12, 256], P('head')
Inputs may be any that keep to these rules, and one draw needn't show every extreme that they name: `memory_flags`: 1 marks a segment with memory.
All inputs are finite; a program needn't handle non-finite values. No bound on the sum of `memory_flags` on one device may be relied on, other than what follows from the above.
Results may differ from a plain program's by a relative error of at most 0.018.
The roundings to bfloat16 on the way count: a program that leaves them out, or rounds other values in their place, can miss the bound.
Values may be sent and summed in bfloat16 or wider, within the bound.
A program may use at most 128 MiB of HBM per device.

v0:
```python
import math
import jax
import jax.numpy as jnp
from jax import lax
from jax.sharding import PartitionSpec as P


def norm_stats(values_in):
    center = values_in - jnp.mean(values_in, axis=-1, keepdims=True)
    factor = lax.rsqrt(jnp.mean(center * center, axis=-1, keepdims=True) + 1e-05)
    return (center * factor, factor)


def norm_back(grad, normed, factor):
    return factor * (
        grad
        - jnp.mean(grad, axis=-1, keepdims=True)
        - normed * jnp.mean(grad * normed, axis=-1, keepdims=True)
    )


def cross_dot(left, right):
    return lax.dot_general(
        left, right, (((0,), (0,)), ((), ())), preferred_element_type=jnp.float32
    )


def back_dot(left, right):
    return lax.dot_general(
        left, right, (((1,), (1,)), ((), ())), preferred_element_type=jnp.float32
    )


def segment_mask(length, bound):
    row_ids = lax.broadcasted_iota(jnp.int32, (length, length), 0)
    col_ids = lax.broadcasted_iota(jnp.int32, (length, length), 1)
    return (col_ids <= row_ids) & ((col_ids >= bound) | (row_ids < bound))


def masked_scores(queries, keys_low, bound):
    factor = queries.shape[-1] ** (-0.5)
    scores = (
        jnp.einsum("qhd,khd->hqk", queries, keys_low, preferred_element_type=jnp.float32) * factor
    )
    return jnp.where(segment_mask(queries.shape[0], bound)[None], scores, -1000000000.0)


def recall_terms(queries, memory_keys, centre_weight, width_weight):
    factor = queries.shape[-1] ** (-0.5)
    mem_scores = (
        jnp.einsum("qhd,nhd->hqn", queries, memory_keys, preferred_element_type=jnp.float32)
        * factor
    )
    centre = jax.nn.sigmoid(
        jnp.einsum("hqn,hn->hq", mem_scores, centre_weight, precision=lax.Precision.HIGHEST)
    )
    width_pre = jnp.einsum("hqn,hn->hq", mem_scores, width_weight, precision=lax.Precision.HIGHEST)
    spread = 0.02 * jax.nn.softplus(width_pre) + 0.01
    basis_count = memory_keys.shape[0]
    centres = (jnp.arange(basis_count, dtype=jnp.float32) + 0.5) / basis_count
    offset = centre[..., None] - centres
    recall = (
        jnp.exp(-offset * offset / (2.0 * spread[..., None]))
        * lax.rsqrt(2.0 * math.pi * spread[..., None])
        / basis_count
    )
    return (mem_scores, centre, width_pre, spread, offset, recall)


def forward_segment(segment_item, centre_weight, width_weight):
    queries, keys_low, values, memory_keys, memory_values, flag, bound = segment_item
    scores = masked_scores(queries, keys_low, bound)
    row_peak = jnp.max(scores, axis=-1, keepdims=True)
    shifted = jnp.exp(scores - row_peak)
    row_total = jnp.sum(shifted, axis=-1, keepdims=True)
    probs_low = (shifted / row_total).astype(jnp.bfloat16)
    local_mix = jnp.einsum("hqk,khd->qhd", probs_low, values, preferred_element_type=jnp.float32)
    recall_low = recall_terms(queries, memory_keys, centre_weight, width_weight)[5].astype(
        jnp.bfloat16
    )
    recalled = jnp.einsum(
        "hqn,nhd->qhd", recall_low, memory_values, preferred_element_type=jnp.float32
    )
    context = (local_mix + flag * recalled).astype(jnp.bfloat16)
    return (context, (row_peak + jnp.log(row_total))[..., 0])


def backward_segment(segment_item, centre_weight, width_weight):
    queries, keys_low, values, memory_keys, memory_values, flag, bound, log_total, grad_context = (
        segment_item
    )
    factor = queries.shape[-1] ** (-0.5)
    scores = masked_scores(queries, keys_low, bound)
    attn_probs = jnp.exp(scores - log_total[..., None])
    probs_low = attn_probs.astype(jnp.bfloat16)
    grad_values = jnp.einsum(
        "hqk,qhd->khd", probs_low, grad_context, preferred_element_type=jnp.float32
    )
    grad_probs = jnp.einsum(
        "qhd,khd->hqk", grad_context, values, preferred_element_type=jnp.float32
    )
    grad_scores = (
        attn_probs * (grad_probs - jnp.sum(attn_probs * grad_probs, axis=-1, keepdims=True))
    ).astype(jnp.bfloat16)
    mem_scores, centre, width_pre, spread, offset, recall = recall_terms(
        queries, memory_keys, centre_weight, width_weight
    )
    recall_low = recall.astype(jnp.bfloat16)
    grad_recall = flag * jnp.einsum(
        "qhd,nhd->hqn", grad_context, memory_values, preferred_element_type=jnp.float32
    )
    memory_value_gradient = flag * jnp.einsum(
        "hqn,qhd->nhd", recall_low, grad_context, preferred_element_type=jnp.float32
    )
    weighted = grad_recall * recall
    spread_b = spread[..., None]
    grad_centre = jnp.sum(weighted * (-offset / spread_b), axis=-1)
    grad_spread = jnp.sum(
        weighted * (offset * offset / (2.0 * spread_b * spread_b) - 0.5 / spread_b), axis=-1
    )
    centre_pre_grad = grad_centre * centre * (1.0 - centre)
    width_pre_grad = grad_spread * 0.02 * jax.nn.sigmoid(width_pre)
    grad_mem_scores = (
        centre_pre_grad[..., None] * centre_weight[:, None, :]
        + width_pre_grad[..., None] * width_weight[:, None, :]
    ).astype(jnp.bfloat16)
    centre_grad = jnp.einsum(
        "hq,hqn->hn", centre_pre_grad, mem_scores, precision=lax.Precision.HIGHEST
    )
    width_grad = jnp.einsum(
        "hq,hqn->hn", width_pre_grad, mem_scores, precision=lax.Precision.HIGHEST
    )
    grad_queries = factor * (
        jnp.einsum("hqk,khd->qhd", grad_scores, keys_low, preferred_element_type=jnp.float32)
        + jnp.einsum(
            "hqn,nhd->qhd", grad_mem_scores, memory_keys, preferred_element_type=jnp.float32
        )
    )
    grad_keys = factor * jnp.einsum(
        "hqk,qhd->khd", grad_scores, queries, preferred_element_type=jnp.float32
    )
    memory_key_gradient = factor * jnp.einsum(
        "hqn,qhd->nhd", grad_mem_scores, queries, preferred_element_type=jnp.float32
    )
    return (
        grad_queries.astype(jnp.bfloat16),
        grad_keys.astype(jnp.bfloat16),
        grad_values.astype(jnp.bfloat16),
        memory_key_gradient.astype(jnp.bfloat16),
        memory_value_gradient.astype(jnp.bfloat16),
        centre_grad,
        width_grad,
    )


def per_device(
    layer_input,
    memory_flags,
    document_start,
    memory_coefficients,
    first_gain,
    first_shift,
    query_weight,
    query_bias,
    key_matrix,
    value_matrix,
    value_offset_bias,
    out_weight,
    out_bias,
    second_gain,
    second_shift,
    up_weight,
    up_bias,
    down_weight,
    down_bias,
    centre_weight,
    width_weight,
    grad_output,
):
    segments = memory_coefficients.shape[0]
    basis_count = memory_coefficients.shape[1]
    group_heads = centre_weight.shape[0]
    group_cols = query_weight.shape[1]
    head_size = group_cols // group_heads
    flag_values = memory_flags.astype(jnp.float32)
    inputs = layer_input.astype(jnp.float32)
    normed_one, factor_one = norm_stats(inputs)
    first_low = (normed_one * first_gain + first_shift).astype(jnp.bfloat16)
    first_rows = lax.all_gather(first_low, "head", axis=0, tiled=True)
    total_rows = first_rows.shape[0]
    length = total_rows // segments
    queries = (
        jnp.dot(first_rows, query_weight, preferred_element_type=jnp.float32) + query_bias
    ).astype(jnp.bfloat16)
    keys_low = jnp.dot(first_rows, key_matrix, preferred_element_type=jnp.float32).astype(
        jnp.bfloat16
    )
    values = (
        jnp.dot(first_rows, value_matrix, preferred_element_type=jnp.float32) + value_offset_bias
    ).astype(jnp.bfloat16)
    memory_keys = jnp.einsum(
        "wmr,rq->wmq", memory_coefficients, key_matrix, preferred_element_type=jnp.float32
    ).astype(jnp.bfloat16)
    memory_values = (
        jnp.einsum(
            "wmr,rq->wmq", memory_coefficients, value_matrix, preferred_element_type=jnp.float32
        )
        + value_offset_bias
    ).astype(jnp.bfloat16)
    tile_shape = (segments, length, group_heads, head_size)
    basis_dimensions = (segments, basis_count, group_heads, head_size)
    seg_items = (
        queries.reshape(tile_shape),
        keys_low.reshape(tile_shape),
        values.reshape(tile_shape),
        memory_keys.reshape(basis_dimensions),
        memory_values.reshape(basis_dimensions),
        flag_values,
        document_start,
    )
    context, log_total = lax.map(
        lambda segment_item: forward_segment(segment_item, centre_weight, width_weight), seg_items
    )
    context = context.reshape(total_rows, group_cols)
    attn_sum = lax.psum_scatter(
        jnp.dot(context, out_weight, preferred_element_type=jnp.float32).astype(jnp.bfloat16),
        "head",
        scatter_dimension=0,
        tiled=True,
    ).astype(jnp.float32)
    hidden = inputs + (attn_sum + out_bias)
    normed_two, factor_two = norm_stats(hidden)
    second_low = (normed_two * second_gain + second_shift).astype(jnp.bfloat16)
    second_rows = lax.all_gather(second_low, "head", axis=0, tiled=True)
    up_pre = jnp.dot(second_rows, up_weight, preferred_element_type=jnp.float32) + up_bias
    up_act = jax.nn.gelu(up_pre, approximate=True).astype(jnp.bfloat16)
    mlp_sum = lax.psum_scatter(
        jnp.dot(up_act, down_weight, preferred_element_type=jnp.float32).astype(jnp.bfloat16),
        "head",
        scatter_dimension=0,
        tiled=True,
    ).astype(jnp.float32)
    layer_output = (hidden + (mlp_sum + down_bias)).astype(jnp.bfloat16)
    down_bias_grad = jnp.sum(grad_output.astype(jnp.float32), axis=0)
    grad_rows = lax.all_gather(grad_output, "head", axis=0, tiled=True)
    down_weight_grad = cross_dot(up_act, grad_rows)
    grad_act = back_dot(grad_rows, down_weight)
    gelu_pull = jax.vjp(lambda values_in: jax.nn.gelu(values_in, approximate=True), up_pre)[1]
    grad_up = gelu_pull(grad_act)[0].astype(jnp.bfloat16)
    up_bias_grad = jnp.sum(grad_up.astype(jnp.float32), axis=0)
    up_weight_grad = cross_dot(second_rows, grad_up)
    grad_second = lax.psum_scatter(
        back_dot(grad_up, up_weight).astype(jnp.bfloat16), "head", scatter_dimension=0, tiled=True
    ).astype(jnp.float32)
    second_gain_grad = jnp.sum(grad_second * normed_two, axis=0)
    second_shift_grad = jnp.sum(grad_second, axis=0)
    grad_hidden = grad_output.astype(jnp.float32) + norm_back(
        grad_second * second_gain, normed_two, factor_two
    )
    branch_low = grad_hidden.astype(jnp.bfloat16)
    out_bias_grad = jnp.sum(branch_low.astype(jnp.float32), axis=0)
    branch_rows = lax.all_gather(branch_low, "head", axis=0, tiled=True)
    out_weight_grad = cross_dot(context, branch_rows)
    grad_context = back_dot(branch_rows, out_weight).astype(jnp.bfloat16)
    back_items = seg_items + (log_total, grad_context.reshape(tile_shape))
    results = lax.map(
        lambda segment_item: backward_segment(segment_item, centre_weight, width_weight), back_items
    )
    grad_queries = results[0].reshape(total_rows, group_cols)
    grad_keys = results[1].reshape(total_rows, group_cols)
    grad_values = results[2].reshape(total_rows, group_cols)
    memory_key_gradient = results[3].reshape(segments, basis_count, group_cols)
    memory_value_gradient = results[4].reshape(segments, basis_count, group_cols)
    centre_weight_grad = jnp.sum(results[5], axis=0)
    width_weight_grad = jnp.sum(results[6], axis=0)
    query_weight_grad = cross_dot(first_rows, grad_queries)
    query_bias_grad = jnp.sum(grad_queries.astype(jnp.float32), axis=0)
    key_weight_grad = cross_dot(first_rows, grad_keys) + jnp.einsum(
        "qwo,qwy->oy", memory_coefficients, memory_key_gradient, preferred_element_type=jnp.float32
    )
    value_weight_grad = cross_dot(first_rows, grad_values) + jnp.einsum(
        "qwo,qwy->oy",
        memory_coefficients,
        memory_value_gradient,
        preferred_element_type=jnp.float32,
    )
    value_bias_grad = jnp.sum(grad_values.astype(jnp.float32), axis=0) + jnp.sum(
        memory_value_gradient.astype(jnp.float32), axis=(0, 1)
    )
    grad_first = lax.psum_scatter(
        (
            back_dot(grad_queries, query_weight)
            + back_dot(grad_keys, key_matrix)
            + back_dot(grad_values, value_matrix)
        ).astype(jnp.bfloat16),
        "head",
        scatter_dimension=0,
        tiled=True,
    ).astype(jnp.float32)
    first_gain_grad = jnp.sum(grad_first * normed_one, axis=0)
    first_shift_grad = jnp.sum(grad_first, axis=0)
    input_grad = (grad_hidden + norm_back(grad_first * first_gain, normed_one, factor_one)).astype(
        jnp.bfloat16
    )
    (
        query_weight_grad,
        query_bias_grad,
        key_weight_grad,
        value_weight_grad,
        value_bias_grad,
        out_weight_grad,
        centre_weight_grad,
        width_weight_grad,
        down_weight_grad,
        up_weight_grad,
        up_bias_grad,
    ) = lax.psum(
        (
            query_weight_grad,
            query_bias_grad,
            key_weight_grad,
            value_weight_grad,
            value_bias_grad,
            out_weight_grad,
            centre_weight_grad,
            width_weight_grad,
            down_weight_grad,
            up_weight_grad,
            up_bias_grad,
        ),
        "batch",
    )
    (
        first_gain_grad,
        first_shift_grad,
        out_bias_grad,
        second_gain_grad,
        second_shift_grad,
        down_bias_grad,
    ) = lax.psum(
        (
            first_gain_grad,
            first_shift_grad,
            out_bias_grad,
            second_gain_grad,
            second_shift_grad,
            down_bias_grad,
        ),
        ("batch", "head"),
    )
    return (
        layer_output,
        input_grad,
        first_gain_grad,
        first_shift_grad,
        query_weight_grad,
        query_bias_grad,
        key_weight_grad,
        value_weight_grad,
        value_bias_grad,
        out_weight_grad,
        out_bias_grad,
        second_gain_grad,
        second_shift_grad,
        up_weight_grad,
        up_bias_grad,
        down_weight_grad,
        down_bias_grad,
        centre_weight_grad,
        width_weight_grad,
    )


def solution(mesh):
    placed = (
        P(("batch", "head"), None),
        P("batch"),
        P("batch"),
        P("batch", None, None),
        P(),
        P(),
        P(None, "head"),
        P("head"),
        P(None, "head"),
        P(None, "head"),
        P("head"),
        P("head", None),
        P(),
        P(),
        P(),
        P(None, "head"),
        P("head"),
        P("head", None),
        P(),
        P("head", None),
        P("head", None),
        P(("batch", "head"), None),
    )
    return jax.shard_map(
        per_device,
        mesh=mesh,
        in_specs=placed,
        out_specs=(
            P(("batch", "head"), None),
            P(("batch", "head"), None),
            P(),
            P(),
            P(None, "head"),
            P("head"),
            P(None, "head"),
            P(None, "head"),
            P("head"),
            P("head", None),
            P(),
            P(),
            P(),
            P(None, "head"),
            P("head"),
            P("head", None),
            P(),
            P("head", None),
            P("head", None),
        ),
        check_vma=False,
    )
```

profile of v0, /device:TPU:0, one launch (start us, length us, event | category | flops | bytes accessed | tf_op | source)
XLA Modules:
  0.0 868.7 jit_solution(15008076573527793442)
XLA Ops:
  14.6 64.0 %all-gather.5.cloned.1.call-done = bf16[2048,768]{1,0:T(8,128)(2,1)} async-done(((bf16[512,768]{1,0:T(8,128)(2,1)}), bf16[2048,768]{1,0:T(8,128)(2,1)}) %all-gather.5.cloned.1.call-update) | async-done | bytes 3145744 | tf_op jit(solution)/shard_map/all_gather | solution.py:189
  78.6 3.1 fusion.166
  84.5 3.9 fusion.165
  88.4 3.1 reshape.257
  91.6 2.2 copy.58
  93.7 4.0 convolution_convert_fusion.4
  97.7 3.0 reshape.259
  100.7 2.2 copy.60
  103.9 54.4 %while.34 = (s32[]{:T(128)}, bf16[4,512,3,64]{1,3,2,0:T(8,128)(2,1)}, f32[4,3,512]{2,1,0:T(4,128)}, bf16[4,512,3,64]{1,3,2,0:T(8,128)(2,1)}, s32[4]{0:T(128)S(1)...) while((s32[]{:T(128)}, ...), condition=%wide.region_5.6_spmd, body=%wide.region_2.5_spmd.sunk | while | flops 325111296 | bytes 17297064 | solution.py:221
  111.6 2.0 fusion.318
  114.3 3.2 fusion.321
  125.2 2.0 fusion.318
  127.9 3.2 fusion.321
  138.8 2.0 fusion.318
  141.5 3.2 fusion.321
  152.4 2.0 fusion.318
  155.0 3.2 fusion.321
  161.1 2.7 convolution_convert_fusion.2
  166.4 56.4 %reduce-scatter.5.cloned.1.call-done = bf16[512,768]{1,0:T(8,128)(2,1)} async-done(((bf16[2048,768]{1,0:T(8,128)(2,1)}), bf16[512,768]{1,0:T(8,128)(2,1)}) %reduce-scatter.5.cloned.1.call-update) | async-done | bytes 786448 | tf_op jit(solution)/shard_map/reduce_scatter | solution.py:225
  228.9 61.8 %all-gather.7.cloned.1.call-done = bf16[2048,768]{1,0:T(8,128)(2,1)} async-done(((bf16[512,768]{1,0:T(8,128)(2,1)}), bf16[2048,768]{1,0:T(8,128)(2,1)}) %all-gather.7.cloned.1.call-update) | async-done | bytes 3145744 | tf_op jit(solution)/shard_map/all_gather | solution.py:234
  290.6 7.5 fusion.196
  298.1 56.1 %all-gather.9.cloned.1.call-done = bf16[2048,768]{1,0:T(8,128)(2,1)} async-done(((bf16[512,768]{1,0:T(8,128)(2,1)}), bf16[2048,768]{1,0:T(8,128)(2,1)}) %all-gather.9.cloned.1.call-update) | async-done | bytes 3145744 | tf_op jit(solution)/shard_map/all_gather | solution.py:245
  354.3 11.0 %convert_reduce_fusion = (f32[768]{0:T(1024)}, bf16[2048,768]{1,0:T(8,128)(2,1)S(1)}, bf16[2048,768]{1,0:T(8,128)(2,1)}) fusion(f32[2048,768]{1,0:T(8,128)} %fusion.196, f32[768]{0:T(1024)} %convert_element_type.193, bf16[2048,768]{1,0:T(8,128)(2,1)} %all-gather.9.cloned.1.call-done, bf16[768,768]{1,0:T(8,128)(2,1)} %param.43), kind=kOutput, calls=%fused_computation.206 | convolution fusion | flops 2455239936 | bytes 16914432 | tf_op jit(solution)/shard_map/dot_general | solution.py:29
  366.9 4.0 convolution_convert_fusion
  371.0 6.5 convolution_convert_fusion.1
  378.8 51.2 %reduce-scatter.9.cloned.1.call-done = bf16[512,768]{1,0:T(8,128)(2,1)} async-done(((bf16[2048,768]{1,0:T(8,128)(2,1)}), bf16[512,768]{1,0:T(8,128)(2,1)}) %reduce-scatter.9.cloned.1.call-update) | async-done | bytes 786448 | tf_op jit(solution)/shard_map/reduce_scatter | solution.py:252
  430.0 2.9 fusion.188
  433.5 59.0 %reduce-scatter.7.cloned.1.call-done = bf16[512,768]{1,0:T(8,128)(2,1)} async-done(((bf16[2048,768]{1,0:T(8,128)(2,1)}), bf16[512,768]{1,0:T(8,128)(2,1)}) %reduce-scatter.7.cloned.1.call-update) | async-done | bytes 786448 | tf_op jit(solution)/shard_map/reduce_scatter | solution.py:237
  492.5 5.3 convert_reduce_fusion.5
  497.8 63.6 %all-gather.11.cloned.1.call-done = bf16[2048,768]{1,0:T(8,128)(2,1)} async-done(((bf16[512,768]{1,0:T(8,128)(2,1)}), bf16[2048,768]{1,0:T(8,128)(2,1)}) %all-gather.11.cloned.1.call-update) | async-done | bytes 3145744 | tf_op jit(solution)/shard_map/all_gather | solution.py:262
  561.4 4.0 convolution_convert_fusion.3
  565.4 3.4 reshape.263
  568.8 2.2 copy.64
  573.9 91.2 %while.35 = (s32[]{:T(128)}, bf16[4,512,3,64]{1,3,2,0:T(8,128)(2,1)}, bf16[4,512,3,64]{1,3,2,0:T(8,128)(2,1)}, bf16[4,512,3,64]{1,3,2,0:T(8,128)(2,1)}, bf16[4,2...) while((s32[]{:T(128)}, ...), condition=%wide.region_17.18_spmd, body=%wide.region_13.17_spmd.sunk | while | flops 795121152 | bytes 42630428 | solution.py:266
  580.1 2.7 fusion.348
  602.8 2.7 fusion.348
  625.6 2.7 fusion.348
  648.4 2.7 fusion.348
  671.7 2.8 add_convert_fusion.3
  674.6 7.1 fusion.201
  681.7 4.2 fusion.200
  701.8 25.6 %all-reduce.1 = (f32[192]{0:T(256)}, f32[192]{0:T(256)}, f32[768]{0:T(1024)}, f32[3,256]{1,0:T(4,128)}, f32[3,256]{1,0:T(4,128)}) all-reduce(f32[192]{0:T(256)} %reduce_sum.229, f32[192]{0:T(256)S(1)} %add.258, f32[768]{0:T(1024)} %get-tuple-element.347, f32[3,256]{1,0:T(4,128)} %reduce_sum.237, ...), channel_id=1, replica_groups=mesh['batch'=8,'head'=4] {'batch'}, use_global_device_ids=true, to_apply=%region_27.28 | all-reduce | flops 2688 | bytes 21504 | tf_op jit(solution)/shard_map/psum | solution.py:317
  727.4 6.2 reduce-scatter.11.cloned.1.call-done
  733.6 2.0 fusion.189
  735.7 41.8 %all-reduce = (f32[768]{0:T(1024)}, f32[768]{0:T(1024)}, f32[768]{0:T(1024)}, f32[768]{0:T(1024)}, f32[768]{0:T(1024)}, /*index=5*/f32[768]{0:T(1024)}) all-reduce(f32[768]{0:T(1024)S(1)} %get-tuple-element.260, f32[768]{0:T(1024)S(1)} %get-tuple-element.265, ...), channel_id=1, replica_groups=mesh['batch'=8,'head'=4] {'batch','head'}, use_global_device_ids=true, to_apply=%region_22.23 | all-reduce | flops 4608 | bytes 36864 | tf_op jit(solution)/shard_map/psum | solution.py:340
  777.5 2.9 fusion.182
  780.4 73.2 %all-reduce.5.cloned.1.call-done = (f32[768,192]{0,1:T(8,128)}, f32[768,192]{0,1:T(8,128)}, f32[768,192]{0,1:T(8,128)}, f32[192,768]{1,0:T(8,128)}, f32[768,768]{1,0:T(8,128)}, /*index=5*/f32[768,768]{1,0:T(8,128)}) async-done(((f32[768,192]{0,1:T(8,128)}, f32[768,192]{0,1:T(8,128)}, f32[768,192]{0,1:T(8,128)}, f32[192,768]{1,0:T(8,128)}, f32[768,768]{1,0:T(8,128)}, /*index=5*/f32[768,768]{1,0:T(8,128)}), ...) | async-done | bytes 7077904 | tf_op jit(solution)/shard_map/psum | solution.py:317
  853.5 2.0 copy.222
  (365 shorter events, 170.6 us)
Async XLA Ops:
  7.2 5.2 copy-start
  7.2 3.8 copy-start.1
  7.2 3.1 copy-start.45
  7.2 3.2 copy-start.46
  7.2 71.4 %all-gather.5.cloned.1.call-start = ((), (), s32[]{:S(2)}) async-start(), calls=%async_computation.4 | async-start | bytes 3932160 | tf_op jit(solution)/shard_map/all_gather | solution.py:189
  8.8 3.6 copy-start.50
  8.8 3.6 copy-start.51
  8.8 3.6 copy-start.52
  8.8 3.6 copy-start.26
  12.3 210.6 %reduce-scatter.5.cloned.1.call-start = ((), (), s32[]{:S(2)}) async-start(), calls=%async_computation.5 | async-start | bytes 3932160 | tf_op jit(solution)/shard_map/reduce_scatter | solution.py:225
  100.7 3.2 copy-start.33
  100.7 3.2 copy-start.34
  100.7 3.2 copy-start.53
  158.3 2.9 copy-start.29
  163.8 126.8 %all-gather.7.cloned.1.call-start = ((), (), s32[]{:S(2)}) async-start(), calls=%async_computation.6 | async-start | bytes 3932160 | tf_op jit(solution)/shard_map/all_gather | solution.py:234
  222.9 2.7 copy-start.43
  227.0 127.3 %all-gather.9.cloned.1.call-start = ((), (), s32[]{:S(2)}) async-start(), calls=%async_computation.8 | async-start | bytes 3932160 | tf_op jit(solution)/shard_map/all_gather | solution.py:245
  227.6 202.4 %reduce-scatter.9.cloned.1.call-start = ((), (), s32[]{:S(2)}) async-start(), calls=%async_computation.9 | async-start | bytes 3932160 | tf_op jit(solution)/shard_map/reduce_scatter | solution.py:252
  354.3 12.6 %copy-start.49 = (bf16[768,768]{1,0:T(8,128)(2,1)S(1)}, bf16[768,768]{1,0:T(8,128)(2,1)}, u32[]{:S(2)}) copy-start(bf16[768,768]{1,0:T(8,128)(2,1)} %param.41) | copy-start | bytes 3538948
  370.9 121.5 %reduce-scatter.7.cloned.1.call-start = ((), (), s32[]{:S(2)}) async-start(), calls=%async_computation.7 | async-start | bytes 3932160 | tf_op jit(solution)/shard_map/reduce_scatter | solution.py:237
  377.5 183.9 %all-gather.11.cloned.1.call-start = ((), (), s32[]{:S(2)}) async-start(), calls=%async_computation.10 | async-start | bytes 3932160 | tf_op jit(solution)/shard_map/all_gather | solution.py:262
  497.8 235.9 %reduce-scatter.11.cloned.1.call-start = ((), (), s32[]{:S(2)}) async-start(), calls=%async_computation.11 | async-start | bytes 3932160 | tf_op jit(solution)/shard_map/reduce_scatter | solution.py:290
  571.0 2.9 copy-start.54
  571.0 2.9 copy-start.56
  577.1 3.0 copy-start.11
  599.8 3.0 copy-start.11
  622.6 3.0 copy-start.11
  645.4 3.0 copy-start.11
  667.2 3.5 copy-start.9
  668.0 3.7 copy-start.12
  674.5 179.0 %all-reduce.5.cloned.1.call-start = ((), (), s32[]{:S(2)}) async-start(), calls=%async_computation.12 | async-start | bytes 14155776 | tf_op jit(solution)/shard_map/psum | solution.py:317
  674.6 7.1 copy-start.48
  674.6 7.1 copy-start.58
  681.7 4.2 copy-start.25
  685.9 2.1 copy-start.16
  688.2 2.1 copy-start.2
  688.2 2.3 copy-start.10
  695.3 6.1 copy-start.15
  695.3 38.3 %copy-start.36 = (f32[768]{0:T(1024)S(1)}, f32[768]{0:T(1024)}, u32[]{:S(2)}) copy-start(f32[768]{0:T(1024)} %copy-done.35) | copy-start | bytes 9220
  695.4 38.3 %copy-start.38 = (f32[512]{0:T(512)S(1)}, f32[512]{0:T(512)}, u32[]{:S(2)}) copy-start(f32[512]{0:T(512)} %copy-done.37) | copy-start | bytes 6148
  695.4 38.3 %copy-start.41 = (f32[512]{0:T(512)S(1)}, f32[512]{0:T(512)}, u32[]{:S(2)}) copy-start(f32[512]{0:T(512)} %copy-done.40) | copy-start | bytes 6148
  700.0 35.7 %copy-start.44 = (f32[768]{0:T(1024)S(1)}, f32[768]{0:T(1024)}, u32[]{:S(2)}) copy-start(f32[768]{0:T(1024)} %get-tuple-element.258) | copy-start | bytes 9220
  733.6 43.9 %copy-start.18 = (bf16[512,768]{1,0:T(8,128)(2,1)S(1)}, bf16[512,768]{1,0:T(8,128)(2,1)}, u32[]{:S(2)}) copy-start(bf16[512,768]{1,0:T(8,128)(2,1)} %reduce-scatter.11.cloned.1.call-done) | copy-start | bytes 2359300
  853.5 2.1 copy-start.24
  853.5 2.9 copy-start.23
  853.5 3.7 copy-start.22
  855.6 2.5 copy-start.20
  858.0 2.5 copy-start.19
  (26 other events, 33.4 us)
Sparse Core Ops, SparseCore 0:
  12.4 66.1 all-gather.4
  163.9 58.8 reduce-scatter.4
  227.1 63.5 all-gather.6
  292.1 62.1 all-gather.8
  371.0 58.8 reduce-scatter.8
  432.1 60.2 reduce-scatter.6
  497.9 63.5 all-gather.10
  674.7 58.8 reduce-scatter.10
  738.8 114.6 all-reduce.4
where the time goes:
time: 874 us; the launch traced here: 869 us
  waiting for transfers between devices  492 us (56%)
  matrix products  186 us (21%)
  blocking collectives  67.4 us (8%)
  local copies, waits for them, and re-layouts  60 us (7%)
  other arithmetic  46.6 us (5%)
  between operations  14.6 us (2%)
    psum x1, waiting for transfers between devices, per_device(): lax.psum((query_weight_grad, query_bias_grad, key_weight_grad, value_weig...  73.2 us
    all_gather x1, waiting for transfers between devices, per_device(): first_rows = lax.all_gather(first_low, 'head', axis=0, tiled=True)  64 us
    all_gather x1, waiting for transfers between devices, per_device(): branch_rows = lax.all_gather(branch_low, 'head', axis=0, tiled=True)  63.6 us
    all_gather x1, waiting for transfers between devices, per_device(): second_rows = lax.all_gather(second_low, 'head', axis=0, tiled=True)  61.8 us
    reduce_scatter x1, waiting for transfers between devices, per_device(): lax.psum_scatter(jnp.dot(up_act, down_weight, preferred_element_type=jnp....  59 us
    reduce_scatter x1, waiting for transfers between devices, per_device(): lax.psum_scatter(jnp.dot(context, out_weight, preferred_element_type=jnp....  56.4 us
    all_gather x1, waiting for transfers between devices, per_device(): grad_rows = lax.all_gather(grad_output, 'head', axis=0, tiled=True)  56.1 us
    reduce_scatter x1, waiting for transfers between devices, per_device(): lax.psum_scatter(back_dot(grad_up, up_weight).astype(jnp.bfloat16), 'head...  51.2 us
  transfers between devices with their start and end apart: 9, of which 9 were waited for; matrix products, arithmetic and copies ran while one was open for 6% of the time, Pallas kernels for 0%

commit v1 on v0

--- a/solution.py
+++ b/solution.py
@@ -186,7 +186,12 @@
     inputs = layer_input.astype(jnp.float32)
     normed_one, factor_one = norm_stats(inputs)
     first_low = (normed_one * first_gain + first_shift).astype(jnp.bfloat16)
-    first_rows = lax.all_gather(first_low, "head", axis=0, tiled=True)
+    ring = [first_low]
+    for hop in range(3):
+        ring.append(lax.ppermute(ring[-1], "head", [(dev, (dev + 1) % 4) for dev in range(4)]))
+    first_rows = jnp.roll(
+        jnp.concatenate(ring[::-1], axis=0), (lax.axis_index("head") + 1) * ring[0].shape[0], axis=0
+    )
     total_rows = first_rows.shape[0]
     length = total_rows // segments
     queries = (

time: 874 us -> 871 us (level)
  waiting for transfers between devices: 492 us -> 482 us
    all_gather x1 -> x0, waiting for transfers between devices: 64 us -> none  [per_device(): first_rows = lax.all_gather(first_low, 'head', axis=0, tiled=True)]
    ppermute x0 -> x3, waiting for transfers between devices: none -> 54.4 us  [per_device(): lax.ppermute(ring[-1], 'head', [(dev, (dev + 1) % 4) for dev in range(4)])]
    unnamed x124 -> x134, local copies, waits for them, and re-layouts: 16.4 us -> 20.3 us
  transfers between devices with their start and end apart: 9 -> 11, of which waited for: 9 -> 11; matrix products, arithmetic and copies ran while one was open for 6% -> 7% of each run, Pallas kernels for 0% -> 0%
where the time goes in v1:
time: 871 us; the launch traced here: 864 us
  waiting for transfers between devices  482 us (55%)
  matrix products  183 us (21%)
  blocking collectives  67.1 us (8%)
  local copies, waits for them, and re-layouts  63.9 us (7%)
  other arithmetic  48 us (6%)
  between operations  15 us (2%)
    psum x1, waiting for transfers between devices, per_device(): lax.psum((query_weight_grad, query_bias_grad, key_weight_grad, value_weig...  73.1 us
    all_gather x1, waiting for transfers between devices, per_device(): branch_rows = lax.all_gather(branch_low, 'head', axis=0, tiled=True)  63.6 us
    all_gather x1, waiting for transfers between devices, per_device(): second_rows = lax.all_gather(second_low, 'head', axis=0, tiled=True)  61.4 us
    reduce_scatter x1, waiting for transfers between devices, per_device(): lax.psum_scatter(jnp.dot(up_act, down_weight, preferred_element_type=jnp....  59 us
    all_gather x1, waiting for transfers between devices, per_device(): grad_rows = lax.all_gather(grad_output, 'head', axis=0, tiled=True)  56.3 us
    reduce_scatter x1, waiting for transfers between devices, per_device(): lax.psum_scatter(jnp.dot(context, out_weight, preferred_element_type=jnp....  55.5 us
    ppermute x3, waiting for transfers between devices, per_device(): lax.ppermute(ring[-1], 'head', [(dev, (dev + 1) % 4) for dev in range(4)])  54.4 us
    reduce_scatter x1, waiting for transfers between devices, per_device(): lax.psum_scatter(back_dot(grad_up, up_weight).astype(jnp.bfloat16), 'head...  51.2 us
  transfers between devices with their start and end apart: 11, of which 11 were waited for; matrix products, arithmetic and copies ran while one was open for 7% of the time, Pallas kernels for 0%

profile of v1, /device:TPU:0, one launch (start us, length us, event | category | flops | bytes accessed | tf_op | source)
XLA Modules:
  0.0 864.3 jit_solution(3114026239799586349)
XLA Ops:
  10.7 3.1 collective-permute-start
  13.8 19.6 %collective-permute-done = bf16[512,768]{1,0:T(8,128)(2,1)S(1)} collective-permute-done((bf16[512,768]{1,0:T(8,128)(2,1)S(1)}, bf16[512,768]{1,0:T(8,128)(2,1)S(1)}, u32[]{:S(2)}, u32[]{:S(2)}) %collective-permute-start) | collective-permute-done | bytes 786464 | tf_op jit(solution)/shard_map/ppermute | solution.py:191
  33.4 20.6 %collective-permute-done.1 = bf16[512,768]{1,0:T(8,128)(2,1)} collective-permute-done((bf16[512,768]{1,0:T(8,128)(2,1)S(1)}, bf16[512,768]{1,0:T(8,128)(2,1)}, u32[]{:S(2)}, u32[]{:S(2)}) %collective-permute-start.1) | collective-permute-done | bytes 786464 | tf_op jit(solution)/shard_map/ppermute | solution.py:191
  57.3 2.4 fusion.205
  59.7 14.2 %collective-permute-done.2 = bf16[512,768]{1,0:T(8,128)(2,1)} collective-permute-done((bf16[512,768]{1,0:T(8,128)(2,1)}, bf16[512,768]{1,0:T(8,128)(2,1)}, u32[]{:S(2)}, u32[]{:S(2)}) %collective-permute-start.2) | collective-permute-done | bytes 786464 | tf_op jit(solution)/shard_map/ppermute | solution.py:191
  80.1 2.6 fusion.165
  82.6 2.0 convolution_convert_fusion.4
  88.6 3.2 reshape.257
  91.8 2.2 copy.58
  94.0 3.0 reshape.259
  96.9 2.2 copy.60
  100.1 54.4 %while.34 = (s32[]{:T(128)}, bf16[4,512,3,64]{1,3,2,0:T(8,128)(2,1)}, f32[4,3,512]{2,1,0:T(4,128)}, bf16[4,512,3,64]{1,3,2,0:T(8,128)(2,1)}, s32[4]{0:T(128)S(1)...) while((s32[]{:T(128)}, ...), condition=%wide.region_5.6_spmd, body=%wide.region_2.5_spmd.sunk | while | flops 325111296 | bytes 17297064 | solution.py:226
  110.5 3.2 fusion.335
  124.1 3.2 fusion.335
  135.1 2.0 fusion.332
  137.7 3.2 fusion.335
  151.3 3.2 fusion.335
  157.4 2.8 convolution_convert_fusion.2
  162.8 55.5 %reduce-scatter.5.cloned.1.call-done = bf16[512,768]{1,0:T(8,128)(2,1)} async-done(((bf16[2048,768]{1,0:T(8,128)(2,1)}), bf16[512,768]{1,0:T(8,128)(2,1)}) %reduce-scatter.5.cloned.1.call-update) | async-done | bytes 786448 | tf_op jit(solution)/shard_map/reduce_scatter | solution.py:230
  224.7 61.4 %all-gather.4.cloned.1.call-done = bf16[2048,768]{1,0:T(8,128)(2,1)} async-done(((bf16[512,768]{1,0:T(8,128)(2,1)}), bf16[2048,768]{1,0:T(8,128)(2,1)}) %all-gather.4.cloned.1.call-update) | async-done | bytes 3145744 | tf_op jit(solution)/shard_map/all_gather | solution.py:239
  286.1 7.5 fusion.217
  293.6 56.3 %all-gather.6.cloned.1.call-done = bf16[2048,768]{1,0:T(8,128)(2,1)} async-done(((bf16[512,768]{1,0:T(8,128)(2,1)}), bf16[2048,768]{1,0:T(8,128)(2,1)}) %all-gather.6.cloned.1.call-update) | async-done | bytes 3145744 | tf_op jit(solution)/shard_map/all_gather | solution.py:250
  349.9 11.0 %convert_reduce_fusion = (f32[768]{0:T(1024)}, bf16[2048,768]{1,0:T(8,128)(2,1)S(1)}, bf16[2048,768]{1,0:T(8,128)(2,1)}) fusion(f32[2048,768]{1,0:T(8,128)} %fusion.217, f32[768]{0:T(1024)} %convert_element_type.193, bf16[2048,768]{1,0:T(8,128)(2,1)} %all-gather.6.cloned.1.call-done, bf16[768,768]{1,0:T(8,128)(2,1)} %param.43), kind=kOutput, calls=%fused_computation.206 | convolution fusion | flops 2455239936 | bytes 16914432 | tf_op jit(solution)/shard_map/dot_general | solution.py:29
  362.5 4.0 convolution_convert_fusion
  366.7 6.5 convolution_convert_fusion.1
  374.5 51.2 %reduce-scatter.9.cloned.1.call-done = bf16[512,768]{1,0:T(8,128)(2,1)} async-done(((bf16[2048,768]{1,0:T(8,128)(2,1)}), bf16[512,768]{1,0:T(8,128)(2,1)}) %reduce-scatter.9.cloned.1.call-update) | async-done | bytes 786448 | tf_op jit(solution)/shard_map/reduce_scatter | solution.py:257
  425.7 2.9 fusion.188
  429.2 59.0 %reduce-scatter.7.cloned.1.call-done = bf16[512,768]{1,0:T(8,128)(2,1)} async-done(((bf16[2048,768]{1,0:T(8,128)(2,1)}), bf16[512,768]{1,0:T(8,128)(2,1)}) %reduce-scatter.7.cloned.1.call-update) | async-done | bytes 786448 | tf_op jit(solution)/shard_map/reduce_scatter | solution.py:242
  488.1 5.3 convert_reduce_fusion.5
  493.5 63.6 %all-gather.8.cloned.1.call-done = bf16[2048,768]{1,0:T(8,128)(2,1)} async-done(((bf16[512,768]{1,0:T(8,128)(2,1)}), bf16[2048,768]{1,0:T(8,128)(2,1)}) %all-gather.8.cloned.1.call-update) | async-done | bytes 3145744 | tf_op jit(solution)/shard_map/all_gather | solution.py:267
  557.1 4.0 convolution_convert_fusion.3
  561.1 3.4 reshape.263
  564.5 2.2 copy.64
  569.6 91.2 %while.35 = (s32[]{:T(128)}, bf16[4,512,3,64]{1,3,2,0:T(8,128)(2,1)}, bf16[4,512,3,64]{1,3,2,0:T(8,128)(2,1)}, bf16[4,512,3,64]{1,3,2,0:T(8,128)(2,1)}, bf16[4,2...) while((s32[]{:T(128)}, ...), condition=%wide.region_17.18_spmd, body=%wide.region_13.17_spmd.sunk | while | flops 795121152 | bytes 42630428 | solution.py:271
  575.7 2.7 fusion.362
  598.5 2.7 fusion.362
  621.2 2.7 fusion.362
  644.0 2.7 fusion.362
  667.1 2.8 add_convert_fusion.3
  669.9 7.1 fusion.222
  677.0 4.2 fusion.221
  696.5 25.3 %all-reduce.1 = (f32[192]{0:T(256)}, f32[192]{0:T(256)}, f32[768]{0:T(1024)}, f32[3,256]{1,0:T(4,128)}, f32[3,256]{1,0:T(4,128)}) all-reduce(f32[192]{0:T(256)} %reduce_sum.229, f32[192]{0:T(256)S(1)} %add.274, f32[768]{0:T(1024)} %get-tuple-element.347, f32[3,256]{1,0:T(4,128)} %reduce_sum.237, ...), channel_id=1, replica_groups=mesh['batch'=8,'head'=4] {'batch'}, use_global_device_ids=true, to_apply=%region_27.28 | all-reduce | flops 2688 | bytes 21504 | tf_op jit(solution)/shard_map/psum | solution.py:322
  721.8 7.1 reduce-scatter.11.cloned.1.call-done
  728.9 2.0 fusion.189
  731.0 41.8 %all-reduce = (f32[768]{0:T(1024)}, f32[768]{0:T(1024)}, f32[768]{0:T(1024)}, f32[768]{0:T(1024)}, f32[768]{0:T(1024)}, /*index=5*/f32[768]{0:T(1024)}) all-reduce(f32[768]{0:T(1024)S(1)} %get-tuple-element.260, f32[768]{0:T(1024)S(1)} %get-tuple-element.265, ...), channel_id=1, replica_groups=mesh['batch'=8,'head'=4] {'batch','head'}, use_global_device_ids=true, to_apply=%region_22.23 | all-reduce | flops 4608 | bytes 36864 | tf_op jit(solution)/shard_map/psum | solution.py:345
  772.8 2.9 fusion.182
  775.7 73.1 %all-reduce.5.cloned.1.call-done = (f32[768,192]{0,1:T(8,128)}, f32[768,192]{0,1:T(8,128)}, f32[768,192]{0,1:T(8,128)}, f32[192,768]{1,0:T(8,128)}, f32[768,768]{1,0:T(8,128)}, /*index=5*/f32[768,768]{1,0:T(8,128)}) async-done(((f32[768,192]{0,1:T(8,128)}, f32[768,192]{0,1:T(8,128)}, f32[768,192]{0,1:T(8,128)}, f32[192,768]{1,0:T(8,128)}, f32[768,768]{1,0:T(8,128)}, /*index=5*/f32[768,768]{1,0:T(8,128)}), ...) | async-done | bytes 7077904 | tf_op jit(solution)/shard_map/psum | solution.py:322
  848.8 2.0 copy.229
  (381 shorter events, 182.9 us)
Async XLA Ops:
  7.2 48.5 %copy-start = (bf16[4,256,768]{2,1,0:T(8,128)(2,1)S(1)}, bf16[4,256,768]{2,1,0:T(8,128)(2,1)}, u32[]{:S(2)}) copy-start(bf16[4,256,768]{2,1,0:T(8,128)(2,1)} %param.29) | copy-start | bytes 4718596
  7.2 3.2 copy-start.1
  7.2 3.1 copy-start.43
  7.2 3.1 copy-start.44
  7.2 46.8 %copy-start.48 = (s32[4]{0:T(128)S(1)}, s32[4]{0:T(128)}, u32[]{:S(2)}) copy-start(s32[4]{0:T(128)} %param.27) | copy-start | bytes 52
  7.2 47.3 %copy-start.49 = (bf16[192]{0:T(256)(128)(2,1)S(1)}, bf16[192]{0:T(256)(128)(2,1)}, u32[]{:S(2)}) copy-start(bf16[192]{0:T(256)(128)(2,1)} %param.36) | copy-start | bytes 1156
  7.3 47.8 %copy-start.50 = (bf16[192]{0:T(256)(128)(2,1)S(1)}, bf16[192]{0:T(256)(128)(2,1)}, u32[]{:S(2)}) copy-start(bf16[192]{0:T(256)(128)(2,1)} %param.33) | copy-start | bytes 1156
  7.3 211.1 %reduce-scatter.5.cloned.1.call-start = ((), (), s32[]{:S(2)}) async-start(), calls=%async_computation.4 | async-start | bytes 3932160 | tf_op jit(solution)/shard_map/reduce_scatter | solution.py:230
  8.8 70.4 %copy-start.35 = (f32[512]{0:T(512)}, f32[512]{0:T(512)S(1)}, u32[]{:S(2)}) copy-start(f32[512]{0:T(512)S(1)} %broadcast_multiply_fusion.7) | copy-start | bytes 6148
  10.3 68.9 %copy-start.37 = (f32[512]{0:T(512)}, f32[512]{0:T(512)S(1)}, u32[]{:S(2)}) copy-start(f32[512]{0:T(512)S(1)} %add_rsqrt_fusion.1) | copy-start | bytes 6148
  10.3 68.9 %copy-start.33 = (f32[768]{0:T(1024)}, f32[768]{0:T(1024)S(1)}, u32[]{:S(2)}) copy-start(f32[768]{0:T(1024)S(1)} %convert_element_type.176) | copy-start | bytes 9220
  10.7 22.6 %collective-permute-start = (bf16[512,768]{1,0:T(8,128)(2,1)S(1)}, bf16[512,768]{1,0:T(8,128)(2,1)S(1)}, u32[]{:S(2)}, u32[]{:S(2)}) collective-permute-start(bf16[512,768]{1,0:T(8,128)(2,1)S(1)} %fusion.178), channel_id=1, source_target_pairs={{0,1},{1,2},{2,3},{3,0},{4,5},{5,6},{6,7},{7,4},{8,9},{9,10},{10,1... | collective-permute-start | bytes 2359304 | tf_op jit(solution)/shard_map/ppermute | solution.py:191
  33.4 20.6 %collective-permute-start.1 = (bf16[512,768]{1,0:T(8,128)(2,1)S(1)}, bf16[512,768]{1,0:T(8,128)(2,1)}, u32[]{:S(2)}, u32[]{:S(2)}) collective-permute-start(bf16[512,768]{1,0:T(8,128)(2,1)S(1)} %collective-permute-done), channel_id=1, source_target_pairs={{0,1},{1,2},{2,3},{3,0},{4,5},{5,6},{6,7},{7,4},{8,9},{9,10},{10,1... | collective-permute-start | bytes 2359304 | tf_op jit(solution)/shard_map/ppermute | solution.py:191
  54.0 19.9 %collective-permute-start.2 = (bf16[512,768]{1,0:T(8,128)(2,1)}, bf16[512,768]{1,0:T(8,128)(2,1)}, u32[]{:S(2)}, u32[]{:S(2)}) collective-permute-start(bf16[512,768]{1,0:T(8,128)(2,1)} %collective-permute-done.1), channel_id=1, source_target_pairs={{0,1},{1,2},{2,3},{3,0},{4,5},{5,6},{6,7},{7,4},{8,9},{9,10},{10,1... | collective-permute-start | bytes 2359304 | tf_op jit(solution)/shard_map/ppermute | solution.py:191
  80.1 4.6 copy-start.4
  96.9 3.2 copy-start.31
  96.9 3.2 copy-start.32
  96.9 3.2 copy-start.51
  96.9 3.2 copy-start.55
  154.5 2.9 copy-start.28
  160.2 125.9 %all-gather.4.cloned.1.call-start = ((), (), s32[]{:S(2)}) async-start(), calls=%async_computation.5 | async-start | bytes 3932160 | tf_op jit(solution)/shard_map/all_gather | solution.py:239
  222.4 127.4 %all-gather.6.cloned.1.call-start = ((), (), s32[]{:S(2)}) async-start(), calls=%async_computation.7 | async-start | bytes 3932160 | tf_op jit(solution)/shard_map/all_gather | solution.py:250
  223.2 202.5 %reduce-scatter.9.cloned.1.call-start = ((), (), s32[]{:S(2)}) async-start(), calls=%async_computation.8 | async-start | bytes 3932160 | tf_op jit(solution)/shard_map/reduce_scatter | solution.py:257
  349.9 12.7 %copy-start.47 = (bf16[768,768]{1,0:T(8,128)(2,1)S(1)}, bf16[768,768]{1,0:T(8,128)(2,1)}, u32[]{:S(2)}) copy-start(bf16[768,768]{1,0:T(8,128)(2,1)} %param.41) | copy-start | bytes 3538948
  366.6 121.5 %reduce-scatter.7.cloned.1.call-start = ((), (), s32[]{:S(2)}) async-start(), calls=%async_computation.6 | async-start | bytes 3932160 | tf_op jit(solution)/shard_map/reduce_scatter | solution.py:242
  373.2 183.9 %all-gather.8.cloned.1.call-start = ((), (), s32[]{:S(2)}) async-start(), calls=%async_computation.9 | async-start | bytes 3932160 | tf_op jit(solution)/shard_map/all_gather | solution.py:267
  493.4 235.5 %reduce-scatter.11.cloned.1.call-start = ((), (), s32[]{:S(2)}) async-start(), calls=%async_computation.10 | async-start | bytes 3932160 | tf_op jit(solution)/shard_map/reduce_scatter | solution.py:295
  566.7 2.9 copy-start.52
  566.7 2.9 copy-start.56
  572.7 3.0 copy-start.9
  595.5 3.0 copy-start.9
  618.2 3.0 copy-start.9
  641.0 3.0 copy-start.9
  663.6 3.4 copy-start.10
  669.9 178.9 %all-reduce.5.cloned.1.call-start = ((), (), s32[]{:S(2)}) async-start(), calls=%async_computation.11 | async-start | bytes 14155776 | tf_op jit(solution)/shard_map/psum | solution.py:322
  669.9 7.1 copy-start.46
  669.9 7.1 copy-start.58
  669.9 12.7 %slice-start = ((s8[6291456]{0:T(1024)(128)(4,1)}), s8[4194304]{0:T(1024)(128)(4,1)S(1)}, s32[]{:S(2)}) async-start(s8[6291456]{0:T(1024)(128)(4,1)} %bitcast.373), calls=%async_computation.12 | async-start | bytes 8388608
  677.0 4.2 copy-start.23
  677.0 5.7 slice-start.1
  690.1 6.1 copy-start.13
  690.1 38.8 %copy-start.34 = (f32[768]{0:T(1024)S(1)}, f32[768]{0:T(1024)}, u32[]{:S(2)}) copy-start(f32[768]{0:T(1024)} %copy-done.33) | copy-start | bytes 9220
  690.1 38.8 %copy-start.36 = (f32[512]{0:T(512)S(1)}, f32[512]{0:T(512)}, u32[]{:S(2)}) copy-start(f32[512]{0:T(512)} %copy-done.35) | copy-start | bytes 6148
  690.1 38.8 %copy-start.38 = (f32[512]{0:T(512)S(1)}, f32[512]{0:T(512)}, u32[]{:S(2)}) copy-start(f32[512]{0:T(512)} %copy-done.37) | copy-start | bytes 6148
  694.7 36.2 %copy-start.42 = (f32[768]{0:T(1024)S(1)}, f32[768]{0:T(1024)}, u32[]{:S(2)}) copy-start(f32[768]{0:T(1024)} %get-tuple-element.258) | copy-start | bytes 9220
  728.9 43.9 %copy-start.16 = (bf16[512,768]{1,0:T(8,128)(2,1)S(1)}, bf16[512,768]{1,0:T(8,128)(2,1)}, u32[]{:S(2)}) copy-start(bf16[512,768]{1,0:T(8,128)(2,1)} %reduce-scatter.11.cloned.1.call-done) | copy-start | bytes 2359300
  848.8 2.9 copy-start.21
  848.8 3.7 copy-start.20
  (30 other events, 47.5 us)
Sparse Core Ops, SparseCore 0:
  160.3 57.9 reduce-scatter.4
  222.5 63.5 all-gather.3
  287.7 62.1 all-gather.5
  366.7 58.8 reduce-scatter.8
  427.8 60.2 reduce-scatter.6
  493.6 63.5 all-gather.7
  670.0 58.8 reduce-scatter.10
  734.1 114.6 all-reduce.4
